TPU v7x, 128 devices: a whole 4x4x4 slice. The times are simulated.
128 devices in a mesh: lat: 8 (over x_lo, y), lon: 16 (over z, x_hi, core).
Axes of the slice: x: 4 (x_hi: 2, x_lo: 2; x = x_hi * 2 + x_lo), y: 4, z: 4, core: 2. Of those that a mesh axis runs over, the one named last changes fastest.
Arguments:
- grad_rows: bfloat16 [131072, 128], P(('lat', 'lon')), may hold values from -6 to 6
- owner: int32 [131072, 1], P(('lat', 'lon')), may hold values from 0 to 127; in each aligned block of 1024 rows (0 to 1023, 1024 to 2047, ...) at most 16 rows name the same one
- lat_offset: int32 [131072], P(('lat', 'lon')), may hold values from 0 to 63
- lon_offset: int32 [131072], P(('lat', 'lon')), may hold values from 0 to 127
- position: bfloat16 [131072, 2], P(('lat', 'lon')), may hold values from 0 to 1
- live_count: int32 [128], P(('lat', 'lon')), may hold values from 512 to 1024
- features: bfloat16 [512, 2048, 128], P('lat', 'lon'), may hold values from -6 to 6
- conv_weight: bfloat16 [3, 3, 128, 128], replicated, may hold values from -0.1875 to 0.1875
Outputs:
- input_grad: bfloat16 [512, 2048, 128], P('lat', 'lon')
- weight_grad: float32 [3, 3, 128, 128], replicated
Inputs may be any that keep to these rules, and one draw needn't show every extreme that they name: `owner`: among the 1024 rows of one device no tile is named more than 16 times, a bound that some block reaches. `live_count`: entry k counts the real rows among the rows of device k, which come first.
All inputs are finite; a program needn't handle non-finite values.
Results may differ from a plain program's by a relative error of at most 0.012.
Values may be sent and summed in bfloat16 or wider, within the bound.
No kernel may reach another device: no remote copies, remote signals or barrier semaphores. Data moves between devices by JAX's collectives and lax.ppermute only.
A program may use at most 128 MiB of HBM per device.

v0:
```python
import math
import jax
import jax.numpy as jnp
from jax import lax
from jax.sharding import PartitionSpec as P

rbf_scale = 1.5


def padded_2(cells, sides, width, closed):
    for axis, dim in sides:
        count = lax.axis_size(axis)
        ends = count if closed else count - 1
        head = lax.slice_in_dim(cells, 0, width, axis=dim)
        tail = lax.slice_in_dim(cells, cells.shape[dim] - width, cells.shape[dim], axis=dim)
        cells = jnp.concatenate(
            [
                lax.ppermute(tail, axis, [(i, (i + 1) % count) for i in range(ends)]),
                cells,
                lax.ppermute(head, axis, [((i + 1) % count, i) for i in range(ends)]),
            ],
            axis=dim,
        )
    return cells


def cut_along(value, dim, count):
    before, after = (value.shape[:dim], value.shape[dim + 1 :])
    return jnp.moveaxis(value.reshape(*before, count, -1, *after), dim, 0)


def in_order(parts, dim):
    shape = list(parts.shape[1:])
    shape[dim] *= parts.shape[0]
    return jnp.moveaxis(parts, 0, dim).reshape(shape)


def one_exchange(value, axis, axes, splits, concats):
    sizes = [lax.axis_size(a) for a in axes]
    parts = cut_along(value, splits[0], sizes[0])
    parts = jnp.moveaxis(cut_along(parts, splits[1] + 1, sizes[1]), 0, 1)
    inside = parts.shape[2:]
    parts = parts.reshape(-1, *inside)
    parts = lax.all_to_all(parts, axis, split_axis=0, concat_axis=0, tiled=True)
    parts = in_order(parts.reshape(*sizes, *inside), concats[0] + 1)
    return in_order(parts, concats[1])


def profile(frac):
    tap_index = jnp.arange(8).astype(frac.dtype)
    return jnp.exp(
        -jnp.square(tap_index[None, :] - 3.0 - frac[:, None]) / (2.0 * rbf_scale * rbf_scale)
    )


def clear_rim(padded):
    lat_index = lax.axis_index("lat")
    lat_count = lax.axis_size("lat")
    row_line = jnp.arange(padded.shape[0], dtype=jnp.int32)
    masked = (row_line == 0) & (lat_index == 0) | (row_line == padded.shape[0] - 1) & (
        lat_index == lat_count - 1
    )
    return jnp.where(masked[:, None, None], jnp.zeros_like(padded), padded)


def tap_matrix(offsets, weights, extent):
    tap_ints = jnp.arange(8, dtype=jnp.int32)
    cells = offsets[:, None] + tap_ints[None, :] + 1
    line = jnp.arange(extent, dtype=jnp.int32)
    picked = jnp.where(
        cells[:, :, None] == line[None, None, :], weights.astype(jnp.float32)[:, :, None], 0.0
    )
    return jnp.sum(picked, axis=1).astype(jnp.bfloat16)


def shards(grad_rows, owner, lat_offset, lon_offset, position, live_count, features, conv_weight):
    lat_total = lax.axis_size("lat")
    lon_total = lax.axis_size("lon")
    device_total = lat_total * lon_total
    row_total = grad_rows.shape[0]
    channels = grad_rows.shape[1]
    tile_lat = features.shape[0]
    tile_lon = features.shape[1]
    capacity = max(2, 2 * row_total // device_total)
    input_padded = clear_rim(padded_2(features, (("lat", 0), ("lon", 1)), 1, True))
    owner_tile = owner[:, 0]
    is_live = jnp.arange(row_total, dtype=jnp.int32) < live_count[0]
    matches = (
        (owner_tile[:, None] == jnp.arange(device_total, dtype=jnp.int32)[None, :])
        & is_live[:, None]
    ).astype(jnp.int32)
    earlier = jnp.cumsum(matches, axis=0) - matches
    slot_rank = jnp.sum(earlier * matches, axis=1)
    slot_index = jnp.where(is_live, owner_tile * capacity + slot_rank, device_total * capacity)
    outgoing = (
        jnp.zeros((device_total * capacity, channels), jnp.bfloat16)
        .at[slot_index]
        .set(grad_rows, mode="drop")
    )
    geometry = jnp.stack(
        [
            position[:, 0],
            position[:, 1],
            lat_offset.astype(jnp.bfloat16),
            lon_offset.astype(jnp.bfloat16),
        ],
        axis=1,
    )
    place_out = (
        jnp.zeros((device_total * capacity, 4), jnp.bfloat16)
        .at[slot_index]
        .set(geometry, mode="drop")
    )
    incoming, place_in = (
        one_exchange(
            outgoing.reshape(lat_total, lon_total, capacity, channels),
            ("lat", "lon"),
            ("lat", "lon"),
            (0, 1),
            (0, 1),
        ),
        one_exchange(
            place_out.reshape(lat_total, lon_total, capacity, 4),
            ("lat", "lon"),
            ("lat", "lon"),
            (0, 1),
            (0, 1),
        ),
    )
    incoming = incoming.reshape(-1, channels)
    place_in = place_in.reshape(-1, 4).astype(jnp.float32)
    padded_lat = tile_lat + 8
    padded_lon = tile_lon + 8
    slot_total = incoming.shape[0]
    block_rows = math.gcd(slot_total, 256)

    def accumulate(canvas, payload):
        rows_blk, place_blk = payload
        lat_weight = profile(place_blk[:, 0]).astype(jnp.bfloat16)
        lon_weight = profile(place_blk[:, 1]).astype(jnp.bfloat16)
        lat_matrix = tap_matrix(place_blk[:, 2].astype(jnp.int32), lat_weight, padded_lat)
        lon_matrix = tap_matrix(place_blk[:, 3].astype(jnp.int32), lon_weight, padded_lon)
        spread = (lon_matrix[:, :, None] * rows_blk[:, None, :]).reshape(
            rows_blk.shape[0], padded_lon * channels
        )
        canvas = canvas + lax.dot_general(
            lat_matrix, spread, (((0,), (0,)), ((), ())), preferred_element_type=jnp.float32
        )
        return (canvas, None)

    canvas, _ = lax.scan(
        accumulate,
        jnp.zeros((padded_lat, padded_lon * channels), jnp.float32),
        (incoming.reshape(-1, block_rows, channels), place_in.reshape(-1, block_rows, 4)),
    )
    canvas = canvas.reshape(padded_lat, padded_lon, channels)
    edge_rows = jnp.concatenate([canvas[:5], canvas[-5:]], axis=0)
    edge_rows = padded_2(edge_rows.astype(jnp.bfloat16), (("lat", 0),), 5, False).astype(
        edge_rows.dtype
    )
    inner = canvas[4:-4]
    inner = inner.at[:4].add(edge_rows[1:5]).at[-4:].add(edge_rows[15:19])
    rim_top = edge_rows[0] + canvas[3]
    rim_bottom = canvas[-4] + edge_rows[19]
    tall = jnp.concatenate([rim_top[None], inner, rim_bottom[None]], axis=0)
    side_cols = jnp.concatenate([tall[:, :5], tall[:, -5:]], axis=1)
    side_cols = padded_2(side_cols.astype(jnp.bfloat16), (("lon", 1),), 5, True).astype(
        side_cols.dtype
    )
    middle = tall[:, 4:-4]
    middle = middle.at[:, :4].add(side_cols[:, 1:5]).at[:, -4:].add(side_cols[:, 15:19])
    rim_left = side_cols[:, 0] + tall[:, 3]
    rim_right = tall[:, -4] + side_cols[:, 19]
    whole = jnp.concatenate([rim_left[:, None], middle, rim_right[:, None]], axis=1)
    grid_padded = clear_rim(whole.astype(jnp.bfloat16))
    grid_grad = grid_padded[1:-1, 1:-1]
    flat_grad = grid_grad.reshape(-1, channels)
    input_grad = jnp.zeros((tile_lat * tile_lon, channels), jnp.float32)
    weight_parts = []
    for a in range(3):
        for b in range(3):
            shifted = grid_padded[2 - a : 2 - a + tile_lat, 2 - b : 2 - b + tile_lon].reshape(
                -1, channels
            )
            input_grad = input_grad + lax.dot_general(
                shifted,
                conv_weight[a, b],
                (((1,), (1,)), ((), ())),
                preferred_element_type=jnp.float32,
            )
            window = input_padded[a : a + tile_lat, b : b + tile_lon].reshape(-1, channels)
            weight_parts.append(
                lax.dot_general(
                    window, flat_grad, (((0,), (0,)), ((), ())), preferred_element_type=jnp.float32
                )
            )
    weight_grad = lax.psum(
        jnp.stack(weight_parts).reshape(3, 3, channels, channels), ("lat", "lon")
    )
    return (input_grad.reshape(tile_lat, tile_lon, channels).astype(jnp.bfloat16), weight_grad)


def solution(mesh):
    placed = (
        P(("lat", "lon"), None),
        P(("lat", "lon"), None),
        P(("lat", "lon")),
        P(("lat", "lon")),
        P(("lat", "lon"), None),
        P(("lat", "lon")),
        P("lat", "lon", None),
        P(),
    )
    return jax.shard_map(
        shards, mesh=mesh, in_specs=placed, out_specs=(P("lat", "lon", None), P()), check_vma=False
    )
```

profile of v0, /device:TPU:1, one launch (start us, length us, event | category | flops | bytes accessed | tf_op | source)
XLA Modules:
  0.0 357.4 jit_solution(9674923736870181824)
XLA Ops:
  8.0 4.5 %collective-permute-start.5 = (bf16[1,128,128]{2,1,0:T(8,128)(2,1)S(1)}, bf16[1,128,128]{2,1,0:T(8,128)(2,1)S(1)}, u32[]{:S(2)}, u32[]{:S(2)}) collective-permute-start(bf16[1,128,128]{2,1,0:T(8,128)(2,1)S(1)} %get-tuple-element.168), channel_id=1, source_target_pairs={{16,0},{32,16},{48,32},{64,48},{80,64},{96,80},{112,96},{0,112},{1... | collective-permute-start | bytes 98312 | tf_op jit(solution)/shard_map/ppermute | solution.py:20
  22.2 11.0 %all-to-all-start = ((bf16[128,1,1,16,4]{3,4,2,1,0:T(4,128)(2,1)}), bf16[128,1,1,16,4]{3,4,2,1,0:T(4,128)(2,1)S(1)}, u32[]{:S(2)}, u32[]{:S(2)}) async-start(bf16[128,1,1,16,4]{3,4,2,1,0:T(4,128)(2,1)} %copy.87), calls=%async_computation | async-start | bytes 262144 | tf_op jit(solution)/shard_map/all_to_all | solution.py:44
  33.2 4.3 %scatter_custom_fusion.1 = bf16[2048,128]{1,0:T(8,128)(2,1)} fusion(s32[1024]{0:T(1024)S(1)} %bitcast.226, bf16[1024,128]{1,0:T(8,128)(2,1)} %param.18, bf16[]{:T(256)} %constant.168.clone.1), kind=kCustom, calls=%fused_computation.87 | custom fusion | bytes 524800 | tf_op jit(solution)/shard_map/scatter | solution.py:98
  37.5 5.6 %all-to-all-done = bf16[128,1,1,16,4]{3,4,2,1,0:T(4,128)(2,1)S(1)} async-done(((bf16[128,1,1,16,4]{3,4,2,1,0:T(4,128)(2,1)}), bf16[128,1,1,16,4]{3,4,2,1,0:T(4,128)(2,1)S(1)}, u32[]{:S(2)}, u32[]{:S(2)}) %all-to-all-start) | async-done | bytes 16416 | tf_op jit(solution)/shard_map/all_to_all | solution.py:44
  43.1 4.2 %all-to-all-start.1 = ((bf16[128,1,1,16,128]{4,3,2,1,0:T(8,128)(2,1)}), bf16[128,1,1,16,128]{4,3,2,1,0:T(8,128)(2,1)S(1)}, u32[]{:S(2)}, u32[]{:S(2)}) async-start(bf16[128,1,1,16,128]{4,3,2,1,0:T(8,128)(2,1)} %bitcast.13), calls=%async_computation.1 | async-start | bytes 1048576 | tf_op jit(solution)/shard_map/all_to_all | solution.py:44
  53.2 8.2 %all-to-all-done.1 = bf16[128,1,1,16,128]{4,3,2,1,0:T(8,128)(2,1)S(1)} async-done(((bf16[128,1,1,16,128]{4,3,2,1,0:T(8,128)(2,1)}), bf16[128,1,1,16,128]{4,3,2,1,0:T(8,128)(2,1)S(1)}, u32[]{:S(2)}, u32[]{:S(2)}) %all-to-all-start.1) | async-done | bytes 524320 | tf_op jit(solution)/shard_map/all_to_all | solution.py:44
  61.4 91.8 %while.17 = (s32[]{:T(128)}, f32[72,17408]{1,0:T(8,128)}, f32[8,256,4]{1,2,0:T(4,128)S(1)}, bf16[8,256,128]{2,1,0:T(8,128)(2,1)S(1)}, s32[]{:T(128)}, /*index=5*/s32[]{:T(128)}) while((s32[]{:T(128)}, f32[72,17408]{1,0:T(8,128)}, f32[8,256,4]{1,2,0:T(4,128)S(1)}, bf16[8,256,128]{2,1,0:T(8,128)(2,1)S(1)}, s32[]{:T(128)}, ...), condition=%wide.region_8.9_spmd.clone, body=%wide.region_5.8_spmd.clone.sunk | while | flops 649949696 | bytes 63582440 | solution.py:151
  61.9 5.2 %broadcast_multiply_fusion.2 = bf16[256,136,128]{2,1,0:T(8,128)(2,1)S(1)} fusion(bf16[256,128]{1,0:T(8,128)(2,1)S(1)} %dynamic-slice_bitcast_fusion.4, bf16[256,136]{1,0:T(8,128)(2,1)S(1)} %copy.129), kind=kLoop, calls=%fused_computation.5.clone.1 | loop fusion | flops 4456448 | bytes 9048064 | tf_op jit(solution)/shard_map/while/body/eval_jaxpr/mul | solution.py:143
  73.4 5.2 %broadcast_multiply_fusion.2 = bf16[256,136,128]{2,1,0:T(8,128)(2,1)S(1)} fusion(bf16[256,128]{1,0:T(8,128)(2,1)S(1)} %dynamic-slice_bitcast_fusion.4, bf16[256,136]{1,0:T(8,128)(2,1)S(1)} %copy.129), kind=kLoop, calls=%fused_computation.5.clone.1 | loop fusion | flops 4456448 | bytes 9048064 | tf_op jit(solution)/shard_map/while/body/eval_jaxpr/mul | solution.py:143
  84.8 5.2 %broadcast_multiply_fusion.2 = bf16[256,136,128]{2,1,0:T(8,128)(2,1)S(1)} fusion(bf16[256,128]{1,0:T(8,128)(2,1)S(1)} %dynamic-slice_bitcast_fusion.4, bf16[256,136]{1,0:T(8,128)(2,1)S(1)} %copy.129), kind=kLoop, calls=%fused_computation.5.clone.1 | loop fusion | flops 4456448 | bytes 9048064 | tf_op jit(solution)/shard_map/while/body/eval_jaxpr/mul | solution.py:143
  90.1 3.6 convolution_add_fusion.10
  96.3 5.2 %broadcast_multiply_fusion.2 = bf16[256,136,128]{2,1,0:T(8,128)(2,1)S(1)} fusion(bf16[256,128]{1,0:T(8,128)(2,1)S(1)} %dynamic-slice_bitcast_fusion.4, bf16[256,136]{1,0:T(8,128)(2,1)S(1)} %copy.129), kind=kLoop, calls=%fused_computation.5.clone.1 | loop fusion | flops 4456448 | bytes 9048064 | tf_op jit(solution)/shard_map/while/body/eval_jaxpr/mul | solution.py:143
  101.5 3.6 convolution_add_fusion.10
  107.8 5.2 %broadcast_multiply_fusion.2 = bf16[256,136,128]{2,1,0:T(8,128)(2,1)S(1)} fusion(bf16[256,128]{1,0:T(8,128)(2,1)S(1)} %dynamic-slice_bitcast_fusion.4, bf16[256,136]{1,0:T(8,128)(2,1)S(1)} %copy.129), kind=kLoop, calls=%fused_computation.5.clone.1 | loop fusion | flops 4456448 | bytes 9048064 | tf_op jit(solution)/shard_map/while/body/eval_jaxpr/mul | solution.py:143
  113.0 3.6 convolution_add_fusion.10
  119.3 5.2 %broadcast_multiply_fusion.2 = bf16[256,136,128]{2,1,0:T(8,128)(2,1)S(1)} fusion(bf16[256,128]{1,0:T(8,128)(2,1)S(1)} %dynamic-slice_bitcast_fusion.4, bf16[256,136]{1,0:T(8,128)(2,1)S(1)} %copy.129), kind=kLoop, calls=%fused_computation.5.clone.1 | loop fusion | flops 4456448 | bytes 9048064 | tf_op jit(solution)/shard_map/while/body/eval_jaxpr/mul | solution.py:143
  124.5 3.6 convolution_add_fusion.10
  130.8 5.2 %broadcast_multiply_fusion.2 = bf16[256,136,128]{2,1,0:T(8,128)(2,1)S(1)} fusion(bf16[256,128]{1,0:T(8,128)(2,1)S(1)} %dynamic-slice_bitcast_fusion.4, bf16[256,136]{1,0:T(8,128)(2,1)S(1)} %copy.129), kind=kLoop, calls=%fused_computation.5.clone.1 | loop fusion | flops 4456448 | bytes 9048064 | tf_op jit(solution)/shard_map/while/body/eval_jaxpr/mul | solution.py:143
  136.0 3.6 convolution_add_fusion.10
  142.2 5.2 %broadcast_multiply_fusion.2 = bf16[256,136,128]{2,1,0:T(8,128)(2,1)S(1)} fusion(bf16[256,128]{1,0:T(8,128)(2,1)S(1)} %dynamic-slice_bitcast_fusion.4, bf16[256,136]{1,0:T(8,128)(2,1)S(1)} %copy.129), kind=kLoop, calls=%fused_computation.5.clone.1 | loop fusion | flops 4456448 | bytes 9048064 | tf_op jit(solution)/shard_map/while/body/eval_jaxpr/mul | solution.py:143
  161.1 4.0 %collective-permute-start = (bf16[5,136,128]{2,1,0:T(8,128)(2,1)S(1)}, bf16[5,136,128]{2,1,0:T(8,128)(2,1)S(1)}, u32[]{:S(2)}, u32[]{:S(2)}) collective-permute-start(bf16[5,136,128]{2,1,0:T(8,128)(2,1)S(1)} %bitcast.203), channel_id=1, source_target_pairs={{0,16},{16,32},{32,48},{48,64},{64,80},{80,96},{96,112},{1,17},{17... | collective-permute-start | bytes 522248 | tf_op jit(solution)/shard_map/ppermute | solution.py:18
  172.8 4.2 %collective-permute-done.3 = bf16[66,5,128]{2,1,0:T(8,128)(2,1)S(1)} collective-permute-done((bf16[66,5,128]{2,1,0:T(8,128)(2,1)S(1)}, bf16[66,5,128]{2,1,0:T(8,128)(2,1)S(1)}, u32[]{:S(2)}, u32[]{:S(2)}) %collective-permute-start.3) | collective-permute-done | bytes 84512 | tf_op jit(solution)/shard_map/ppermute | solution.py:20
  181.1 7.0 %fusion.129 = (bf16[64,128,128]{2,1,0:T(8,128)(2,1)}, bf16[64,128,128]{2,1,0:T(8,128)(2,1)S(1)}, bf16[64,128,128]{2,1,0:T(8,128)(2,1)}, bf16[64,128,128]{2,1,0:T...) fusion(bf16[66,130,128]{2,1,0:T(8,128)(2,1)S(1)} %get-tuple-ele, ...), kind=kLoop, calls=%fused_computation.153 | loop fusion | bytes 37748736 | tf_op jit(solution)/shard_map/slice | solution.py:182
  214.3 134.3 %all-reduce.2.cloned.1.call-done = f32[3,3,128,128]{3,2,1,0:T(8,128)} async-done(((f32[3,3,128,128]{3,2,1,0:T(8,128)}), f32[3,3,128,128]{3,2,1,0:T(8,128)}) %all-reduce.2.cloned.1.call-update) | async-done | bytes 589840 | tf_op jit(solution)/shard_map/psum | solution.py:197
  (245 shorter events, 94.9 us)
Async XLA Ops:
  7.2 9.6 %copy-start.11 = (s32[1024,1]{0,1:T(1,128)S(1)}, s32[1024,1]{0,1:T(1,128)}, u32[]{:S(2)}) copy-start(s32[1024,1]{0,1:T(1,128)} %param.19) | copy-start | bytes 12292
  8.0 41.9 %collective-permute-start.5 = (bf16[1,128,128]{2,1,0:T(8,128)(2,1)S(1)}, bf16[1,128,128]{2,1,0:T(8,128)(2,1)S(1)}, u32[]{:S(2)}, u32[]{:S(2)}) collective-permute-start(bf16[1,128,128]{2,1,0:T(8,128)(2,1)S(1)} %get-tuple-element.168), channel_id=1, source_target_pairs={{16,0},{32,16},{48,32},{64,48},{80,64},{96,80},{112,96},{0,112},{1... | collective-permute-start | bytes 98312 | tf_op jit(solution)/shard_map/ppermute | solution.py:20
  12.5 35.4 %collective-permute-start.4 = (bf16[1,128,128]{2,1,0:T(8,128)(2,1)S(1)}, bf16[1,128,128]{2,1,0:T(8,128)(2,1)S(1)}, u32[]{:S(2)}, u32[]{:S(2)}) collective-permute-start(bf16[1,128,128]{2,1,0:T(8,128)(2,1)S(1)} %get-tuple-element.169), channel_id=1, source_target_pairs={{0,16},{16,32},{32,48},{48,64},{64,80},{80,96},{96,112},{112,0},{1... | collective-permute-start | bytes 98312 | tf_op jit(solution)/shard_map/ppermute | solution.py:18
  22.2 20.9 %all-to-all-start = ((bf16[128,1,1,16,4]{3,4,2,1,0:T(4,128)(2,1)}), bf16[128,1,1,16,4]{3,4,2,1,0:T(4,128)(2,1)S(1)}, u32[]{:S(2)}, u32[]{:S(2)}) async-start(bf16[128,1,1,16,4]{3,4,2,1,0:T(4,128)(2,1)} %copy.87), calls=%async_computation | async-start | bytes 262144 | tf_op jit(solution)/shard_map/all_to_all | solution.py:44
  43.1 18.3 %all-to-all-start.1 = ((bf16[128,1,1,16,128]{4,3,2,1,0:T(8,128)(2,1)}), bf16[128,1,1,16,128]{4,3,2,1,0:T(8,128)(2,1)S(1)}, u32[]{:S(2)}, u32[]{:S(2)}) async-start(bf16[128,1,1,16,128]{4,3,2,1,0:T(8,128)(2,1)} %bitcast.13), calls=%async_computation.1 | async-start | bytes 1048576 | tf_op jit(solution)/shard_map/all_to_all | solution.py:44
  47.3 301.3 %all-reduce.2.cloned.1.call-start = ((), (), s32[]{:S(2)}) async-start(), calls=%async_computation.2 | async-start | bytes 1179648 | tf_op jit(solution)/shard_map/psum | solution.py:197
  50.0 128.0 %collective-permute-start.6 = (bf16[66,1,128]{2,1,0:T(2,128)(2,1)S(1)}, bf16[66,1,128]{2,1,0:T(2,128)(2,1)S(1)}, u32[]{:S(2)}, u32[]{:S(2)}) collective-permute-start(bf16[66,1,128]{2,1,0:T(2,128)(2,1)S(1)} %get-tuple-element.166), channel_id=1, source_target_pairs={{0,1},{1,2},{2,3},{3,4},{4,5},{5,6},{6,7},{7,8},{8,9},{9,10},{10,1... | collective-permute-start | bytes 50696 | tf_op jit(solution)/shard_map/ppermute | solution.py:18
  53.2 124.8 %collective-permute-start.7 = (bf16[66,1,128]{2,1,0:T(2,128)(2,1)S(1)}, bf16[66,1,128]{2,1,0:T(2,128)(2,1)S(1)}, u32[]{:S(2)}, u32[]{:S(2)}) collective-permute-start(bf16[66,1,128]{2,1,0:T(2,128)(2,1)S(1)} %get-tuple-element.167), channel_id=1, source_target_pairs={{1,0},{2,1},{3,2},{4,3},{5,4},{6,5},{7,6},{8,7},{9,8},{10,9},{11,1... | collective-permute-start | bytes 50696 | tf_op jit(solution)/shard_map/ppermute | solution.py:20
  61.8 5.2 %slice-start = ((s8[5013504]{0:T(1024)(128)(4,1)}), s8[4194304]{0:T(1024)(128)(4,1)S(1)}, s32[]{:S(2)}) async-start(s8[5013504]{0:T(1024)(128)(4,1)} %bitcast.191), calls=%async_computation.3 | async-start | bytes 8388608 | tf_op jit(solution)/shard_map/while
  61.9 5.2 %slice-start.1 = ((s8[5013504]{0:T(1024)(128)(4,1)}), s8[819200]{0:T(1024)(128)(4,1)S(1)}, s32[]{:S(2)}) async-start(s8[5013504]{0:T(1024)(128)(4,1)} %bitcast.191), calls=%async_computation.4 | async-start | bytes 1638400 | tf_op jit(solution)/shard_map/while
  73.3 5.2 %slice-start = ((s8[5013504]{0:T(1024)(128)(4,1)}), s8[4194304]{0:T(1024)(128)(4,1)S(1)}, s32[]{:S(2)}) async-start(s8[5013504]{0:T(1024)(128)(4,1)} %bitcast.191), calls=%async_computation.3 | async-start | bytes 8388608 | tf_op jit(solution)/shard_map/while
  73.4 5.2 %slice-start.1 = ((s8[5013504]{0:T(1024)(128)(4,1)}), s8[819200]{0:T(1024)(128)(4,1)S(1)}, s32[]{:S(2)}) async-start(s8[5013504]{0:T(1024)(128)(4,1)} %bitcast.191), calls=%async_computation.4 | async-start | bytes 1638400 | tf_op jit(solution)/shard_map/while
  84.8 5.2 %slice-start = ((s8[5013504]{0:T(1024)(128)(4,1)}), s8[4194304]{0:T(1024)(128)(4,1)S(1)}, s32[]{:S(2)}) async-start(s8[5013504]{0:T(1024)(128)(4,1)} %bitcast.191), calls=%async_computation.3 | async-start | bytes 8388608 | tf_op jit(solution)/shard_map/while
  84.8 5.2 %slice-start.1 = ((s8[5013504]{0:T(1024)(128)(4,1)}), s8[819200]{0:T(1024)(128)(4,1)S(1)}, s32[]{:S(2)}) async-start(s8[5013504]{0:T(1024)(128)(4,1)} %bitcast.191), calls=%async_computation.4 | async-start | bytes 1638400 | tf_op jit(solution)/shard_map/while
  96.3 5.2 %slice-start = ((s8[5013504]{0:T(1024)(128)(4,1)}), s8[4194304]{0:T(1024)(128)(4,1)S(1)}, s32[]{:S(2)}) async-start(s8[5013504]{0:T(1024)(128)(4,1)} %bitcast.191), calls=%async_computation.3 | async-start | bytes 8388608 | tf_op jit(solution)/shard_map/while
  107.8 5.2 %slice-start = ((s8[5013504]{0:T(1024)(128)(4,1)}), s8[4194304]{0:T(1024)(128)(4,1)S(1)}, s32[]{:S(2)}) async-start(s8[5013504]{0:T(1024)(128)(4,1)} %bitcast.191), calls=%async_computation.3 | async-start | bytes 8388608 | tf_op jit(solution)/shard_map/while
  119.2 5.2 %slice-start = ((s8[5013504]{0:T(1024)(128)(4,1)}), s8[4194304]{0:T(1024)(128)(4,1)S(1)}, s32[]{:S(2)}) async-start(s8[5013504]{0:T(1024)(128)(4,1)} %bitcast.191), calls=%async_computation.3 | async-start | bytes 8388608 | tf_op jit(solution)/shard_map/while
  119.3 5.2 %slice-start.1 = ((s8[5013504]{0:T(1024)(128)(4,1)}), s8[819200]{0:T(1024)(128)(4,1)S(1)}, s32[]{:S(2)}) async-start(s8[5013504]{0:T(1024)(128)(4,1)} %bitcast.191), calls=%async_computation.4 | async-start | bytes 1638400 | tf_op jit(solution)/shard_map/while
  130.7 5.2 %slice-start = ((s8[5013504]{0:T(1024)(128)(4,1)}), s8[4194304]{0:T(1024)(128)(4,1)S(1)}, s32[]{:S(2)}) async-start(s8[5013504]{0:T(1024)(128)(4,1)} %bitcast.191), calls=%async_computation.3 | async-start | bytes 8388608 | tf_op jit(solution)/shard_map/while
  142.2 5.2 %slice-start = ((s8[5013504]{0:T(1024)(128)(4,1)}), s8[4194304]{0:T(1024)(128)(4,1)S(1)}, s32[]{:S(2)}) async-start(s8[5013504]{0:T(1024)(128)(4,1)} %bitcast.191), calls=%async_computation.3 | async-start | bytes 8388608 | tf_op jit(solution)/shard_map/while
  159.8 7.7 %collective-permute-start.1 = (bf16[5,136,128]{2,1,0:T(8,128)(2,1)S(1)}, bf16[5,136,128]{2,1,0:T(8,128)(2,1)S(1)}, u32[]{:S(2)}, u32[]{:S(2)}) collective-permute-start(bf16[5,136,128]{2,1,0:T(8,128)(2,1)S(1)} %bitcast.207), channel_id=1, source_target_pairs={{16,0},{32,16},{48,32},{64,48},{80,64},{96,80},{112,96},{17,1},{33... | collective-permute-start | bytes 522248 | tf_op jit(solution)/shard_map/ppermute | solution.py:20
  161.1 7.2 %collective-permute-start = (bf16[5,136,128]{2,1,0:T(8,128)(2,1)S(1)}, bf16[5,136,128]{2,1,0:T(8,128)(2,1)S(1)}, u32[]{:S(2)}, u32[]{:S(2)}) collective-permute-start(bf16[5,136,128]{2,1,0:T(8,128)(2,1)S(1)} %bitcast.203), channel_id=1, source_target_pairs={{0,16},{16,32},{32,48},{48,64},{64,80},{80,96},{96,112},{1,17},{17... | collective-permute-start | bytes 522248 | tf_op jit(solution)/shard_map/ppermute | solution.py:18
  168.8 3.9 %collective-permute-start.2 = (bf16[66,5,128]{2,1,0:T(8,128)(2,1)S(1)}, bf16[66,5,128]{2,1,0:T(8,128)(2,1)S(1)}, u32[]{:S(2)}, u32[]{:S(2)}) collective-permute-start(bf16[66,5,128]{2,1,0:T(8,128)(2,1)S(1)} %get-tuple-element.164), channel_id=1, source_target_pairs={{0,1},{1,2},{2,3},{3,4},{4,5},{5,6},{6,7},{7,8},{8,9},{9,10},{10,1... | collective-permute-start | bytes 253448 | tf_op jit(solution)/shard_map/ppermute | solution.py:18
  170.8 6.2 %collective-permute-start.3 = (bf16[66,5,128]{2,1,0:T(8,128)(2,1)S(1)}, bf16[66,5,128]{2,1,0:T(8,128)(2,1)S(1)}, u32[]{:S(2)}, u32[]{:S(2)}) collective-permute-start(bf16[66,5,128]{2,1,0:T(8,128)(2,1)S(1)} %get-tuple-element.165), channel_id=1, source_target_pairs={{1,0},{2,1},{3,2},{4,3},{5,4},{6,5},{7,6},{8,7},{9,8},{10,9},{11,1... | collective-permute-start | bytes 253448 | tf_op jit(solution)/shard_map/ppermute | solution.py:20
  (22 other events, 57.7 us)
Sparse Core Ops, SparseCore 0:
  199.6 148.9 all-reduce.1
where the time goes:
time: 358 us; the launch traced here: 357 us
  waiting for transfers between devices  157 us (44%)
  other arithmetic  54.3 us (15%)
  local copies, waits for them, and re-layouts  51.6 us (14%)
  matrix products  48.7 us (14%)
  starting transfers between devices  30.1 us (8%)
  between operations  15.2 us (4%)
    psum x1, waiting for transfers between devices, shards(): lax.psum(jnp.stack(weight_parts).reshape(3, 3, channels, channels), ('lat...  134 us
    mul x8, other arithmetic, accumulate(): lon_matrix[:, :, None] * rows_blk[:, None, :]  41.4 us
    dot_general x8, matrix products, accumulate(): lax.dot_general(lat_matrix, spread, (((0,), (0,)), ((), ())), preferred_e...  28.5 us
    while x48, local copies, waits for them, and re-layouts  17.9 us
    all_to_all x2, starting transfers between devices, one_exchange(): parts = lax.all_to_all(parts, axis, split_axis=0, concat_axis=0, tiled=True)  15.1 us
    all_to_all x2, waiting for transfers between devices, one_exchange(): parts = lax.all_to_all(parts, axis, split_axis=0, concat_axis=0, tiled=True)  13.8 us
    unnamed x33, local copies, waits for them, and re-layouts  12.4 us
    dot_general x9, matrix products, shards(): lax.dot_general(window, flat_grad, (((0,), (0,)), ((), ())), preferred_el...  10.5 us
  transfers between devices with their start and end apart: 11, of which 7 were waited for; matrix products, arithmetic and copies ran while one was open for 30% of the time, Pallas kernels for 0%

commit v1 on v0

--- a/solution.py
+++ b/solution.py
@@ -194,8 +194,9 @@
                     window, flat_grad, (((0,), (0,)), ((), ())), preferred_element_type=jnp.float32
                 )
             )
-    weight_grad = lax.psum(
-        jnp.stack(weight_parts).reshape(3, 3, channels, channels), ("lat", "lon")
+    weight_grad = jnp.sum(
+        lax.all_gather(jnp.stack(weight_parts).reshape(3, 3, channels, channels), ("lat", "lon")),
+        axis=0,
     )
     return (input_grad.reshape(tile_lat, tile_lon, channels).astype(jnp.bfloat16), weight_grad)
 

time: 358 us -> 673 us (1.88)
  waiting for transfers between devices: 157 us -> 416 us
  matrix products: 48.7 us -> 90.9 us
  other arithmetic: 54.3 us -> 93.8 us
  local copies, waits for them, and re-layouts: 51.6 us -> 27.1 us
    all_gather x0 -> x1, waiting for transfers between devices: none -> 397 us  [shards(): lax.all_gather(jnp.stack(weight_parts).reshape(3, 3, channels, channels),...]
    psum x1 -> x0, waiting for transfers between devices: 134 us -> none  [shards(): lax.psum(jnp.stack(weight_parts).reshape(3, 3, channels, channels), ('lat...]
    dot_general x8, matrix products: 28.5 us -> 71.1 us  [accumulate(): lax.dot_general(lat_matrix, spread, (((0,), (0,)), ((), ())), preferred_e...]
    reduce_sum x0 -> x1, other arithmetic: none -> 24.1 us  [shards(): jnp.sum(lax.all_gather(jnp.stack(weight_parts).reshape(3, 3, channels, ch...]
    while x48 -> x0, local copies, waits for them, and re-layouts: 17.9 us -> none
    mul x8, other arithmetic: 41.4 us -> 58.9 us  [accumulate(): lon_matrix[:, :, None] * rows_blk[:, None, :]]
  transfers between devices with their start and end apart: 11 -> 11, of which waited for: 7 -> 6; matrix products, arithmetic and copies ran while one was open for 30% -> 25% of each run, Pallas kernels for 0% -> 0%
where the time goes in v1:
time: 673 us
  waiting for transfers between devices  416 us (62%)
  other arithmetic  93.8 us (14%)
  matrix products  90.9 us (14%)
  starting transfers between devices  29.7 us (4%)
  local copies, waits for them, and re-layouts  27.1 us (4%)
  between operations  15.3 us (2%)
    all_gather x1, waiting for transfers between devices, shards(): lax.all_gather(jnp.stack(weight_parts).reshape(3, 3, channels, channels),...  397 us
    dot_general x8, matrix products, accumulate(): lax.dot_general(lat_matrix, spread, (((0,), (0,)), ((), ())), preferred_e...  71.1 us
    mul x8, other arithmetic, accumulate(): lon_matrix[:, :, None] * rows_blk[:, None, :]  58.9 us
    reduce_sum x1, other arithmetic, shards(): jnp.sum(lax.all_gather(jnp.stack(weight_parts).reshape(3, 3, channels, ch...  24.1 us
    all_to_all x2, waiting for transfers between devices, one_exchange(): parts = lax.all_to_all(parts, axis, split_axis=0, concat_axis=0, tiled=True)  13.8 us
  transfers between devices with their start and end apart: 11, of which 6 were waited for; matrix products, arithmetic and copies ran while one was open for 25% of the time, Pallas kernels for 0%

profile of v1, /device:TPU:1, one launch (start us, length us, event | category | flops | bytes accessed | tf_op | source)
XLA Modules:
  0.0 672.8 jit_solution(3007490856975138957)
XLA Ops:
  20.3 9.0 %all-to-all-start = ((bf16[128,1,1,16,4]{3,4,2,1,0:T(4,128)(2,1)}), bf16[128,1,1,16,4]{3,4,2,1,0:T(4,128)(2,1)S(1)}, u32[]{:S(2)}, u32[]{:S(2)}) async-start(bf16[128,1,1,16,4]{3,4,2,1,0:T(4,128)(2,1)} %copy.87), calls=%async_computation | async-start | bytes 262144 | tf_op jit(solution)/shard_map/all_to_all | solution.py:44
  29.3 4.3 scatter_custom_fusion.1
  33.6 5.6 all-to-all-done
  49.1 8.2 %all-to-all-done.1 = bf16[128,1,1,16,128]{4,3,2,1,0:T(8,128)(2,1)S(1)} async-done(((bf16[128,1,1,16,128]{4,3,2,1,0:T(8,128)(2,1)}), bf16[128,1,1,16,128]{4,3,2,1,0:T(8,128)(2,1)S(1)}, u32[]{:S(2)}, u32[]{:S(2)}) %all-to-all-start.1) | async-done | bytes 524320 | tf_op jit(solution)/shard_map/all_to_all | solution.py:44
  57.3 133.4 %while.17 = (s32[]{:T(128)}, f32[72,17408]{1,0:T(8,128)}, f32[8,256,4]{1,2,0:T(4,128)S(1)}, bf16[8,256,128]{2,1,0:T(8,128)(2,1)S(1)}, s32[]{:T(128)}, /*index=5*/s32[]{:T(128)}) while((s32[]{:T(128)}, f32[72,17408]{1,0:T(8,128)}, f32[8,256,4]{1,2,0:T(4,128)S(1)}, bf16[8,256,128]{2,1,0:T(8,128)(2,1)S(1)}, s32[]{:T(128)}, ...), condition=%wide.region_8.9_spmd.clone, body=%wide.region_5.8_spmd.clone.sunk | while | flops 649949696 | bytes 28487836 | solution.py:151
  57.6 7.4 %broadcast_multiply_fusion.2 = bf16[256,136,128]{2,1,0:T(8,128)(2,1)} fusion(bf16[256,128]{1,0:T(8,128)(2,1)S(1)} %dynamic-slice_bitcast_fusion.4, bf16[256,136]{1,0:T(8,128)(2,1)S(1)} %copy.129), kind=kLoop, calls=%fused_computation.5.clone.1 | loop fusion | flops 4456448 | bytes 9048064 | tf_op jit(solution)/shard_map/while/body/eval_jaxpr/mul | solution.py:143
  65.1 7.6 %convolution_add_fusion.10 = f32[72,17408]{1,0:T(8,128)} fusion(bf16[32,8,136,128]{3,2,1,0:T(8,128)(2,1)} %bitcast.188, f32[72,17408]{1,0:T(8,128)} %get-tuple-element.218, pred[]{:T(512)S(6)} %compare.25, bf16[256,72]{0,1:T(8,128)(2,1)S(1)} %select_reduce_fusion.5), kind=kOutput, calls=%fused_computation.2.clone.1 | convolution fusion | flops 644235264 | bytes 18976768 | tf_op jit(solution)/shard_map/while/body/eval_jaxpr/dot_general | solution.py:146
  73.1 7.4 %broadcast_multiply_fusion.2 = bf16[256,136,128]{2,1,0:T(8,128)(2,1)} fusion(bf16[256,128]{1,0:T(8,128)(2,1)S(1)} %dynamic-slice_bitcast_fusion.4, bf16[256,136]{1,0:T(8,128)(2,1)S(1)} %copy.129), kind=kLoop, calls=%fused_computation.5.clone.1 | loop fusion | flops 4456448 | bytes 9048064 | tf_op jit(solution)/shard_map/while/body/eval_jaxpr/mul | solution.py:143
  80.5 9.1 %convolution_add_fusion.10 = f32[72,17408]{1,0:T(8,128)} fusion(bf16[32,8,136,128]{3,2,1,0:T(8,128)(2,1)} %bitcast.188, f32[72,17408]{1,0:T(8,128)} %get-tuple-element.218, pred[]{:T(512)S(6)} %compare.25, bf16[256,72]{0,1:T(8,128)(2,1)S(1)} %select_reduce_fusion.5), kind=kOutput, calls=%fused_computation.2.clone.1 | convolution fusion | flops 644235264 | bytes 18976768 | tf_op jit(solution)/shard_map/while/body/eval_jaxpr/dot_general | solution.py:146
  89.9 7.4 %broadcast_multiply_fusion.2 = bf16[256,136,128]{2,1,0:T(8,128)(2,1)} fusion(bf16[256,128]{1,0:T(8,128)(2,1)S(1)} %dynamic-slice_bitcast_fusion.4, bf16[256,136]{1,0:T(8,128)(2,1)S(1)} %copy.129), kind=kLoop, calls=%fused_computation.5.clone.1 | loop fusion | flops 4456448 | bytes 9048064 | tf_op jit(solution)/shard_map/while/body/eval_jaxpr/mul | solution.py:143
  97.4 9.1 %convolution_add_fusion.10 = f32[72,17408]{1,0:T(8,128)} fusion(bf16[32,8,136,128]{3,2,1,0:T(8,128)(2,1)} %bitcast.188, f32[72,17408]{1,0:T(8,128)} %get-tuple-element.218, pred[]{:T(512)S(6)} %compare.25, bf16[256,72]{0,1:T(8,128)(2,1)S(1)} %select_reduce_fusion.5), kind=kOutput, calls=%fused_computation.2.clone.1 | convolution fusion | flops 644235264 | bytes 18976768 | tf_op jit(solution)/shard_map/while/body/eval_jaxpr/dot_general | solution.py:146
  106.8 7.4 %broadcast_multiply_fusion.2 = bf16[256,136,128]{2,1,0:T(8,128)(2,1)} fusion(bf16[256,128]{1,0:T(8,128)(2,1)S(1)} %dynamic-slice_bitcast_fusion.4, bf16[256,136]{1,0:T(8,128)(2,1)S(1)} %copy.129), kind=kLoop, calls=%fused_computation.5.clone.1 | loop fusion | flops 4456448 | bytes 9048064 | tf_op jit(solution)/shard_map/while/body/eval_jaxpr/mul | solution.py:143
  114.2 9.1 %convolution_add_fusion.10 = f32[72,17408]{1,0:T(8,128)} fusion(bf16[32,8,136,128]{3,2,1,0:T(8,128)(2,1)} %bitcast.188, f32[72,17408]{1,0:T(8,128)} %get-tuple-element.218, pred[]{:T(512)S(6)} %compare.25, bf16[256,72]{0,1:T(8,128)(2,1)S(1)} %select_reduce_fusion.5), kind=kOutput, calls=%fused_computation.2.clone.1 | convolution fusion | flops 644235264 | bytes 18976768 | tf_op jit(solution)/shard_map/while/body/eval_jaxpr/dot_general | solution.py:146
  123.6 7.4 %broadcast_multiply_fusion.2 = bf16[256,136,128]{2,1,0:T(8,128)(2,1)} fusion(bf16[256,128]{1,0:T(8,128)(2,1)S(1)} %dynamic-slice_bitcast_fusion.4, bf16[256,136]{1,0:T(8,128)(2,1)S(1)} %copy.129), kind=kLoop, calls=%fused_computation.5.clone.1 | loop fusion | flops 4456448 | bytes 9048064 | tf_op jit(solution)/shard_map/while/body/eval_jaxpr/mul | solution.py:143
  131.1 9.1 %convolution_add_fusion.10 = f32[72,17408]{1,0:T(8,128)} fusion(bf16[32,8,136,128]{3,2,1,0:T(8,128)(2,1)} %bitcast.188, f32[72,17408]{1,0:T(8,128)} %get-tuple-element.218, pred[]{:T(512)S(6)} %compare.25, bf16[256,72]{0,1:T(8,128)(2,1)S(1)} %select_reduce_fusion.5), kind=kOutput, calls=%fused_computation.2.clone.1 | convolution fusion | flops 644235264 | bytes 18976768 | tf_op jit(solution)/shard_map/while/body/eval_jaxpr/dot_general | solution.py:146
  140.5 7.4 %broadcast_multiply_fusion.2 = bf16[256,136,128]{2,1,0:T(8,128)(2,1)} fusion(bf16[256,128]{1,0:T(8,128)(2,1)S(1)} %dynamic-slice_bitcast_fusion.4, bf16[256,136]{1,0:T(8,128)(2,1)S(1)} %copy.129), kind=kLoop, calls=%fused_computation.5.clone.1 | loop fusion | flops 4456448 | bytes 9048064 | tf_op jit(solution)/shard_map/while/body/eval_jaxpr/mul | solution.py:143
  147.9 9.1 %convolution_add_fusion.10 = f32[72,17408]{1,0:T(8,128)} fusion(bf16[32,8,136,128]{3,2,1,0:T(8,128)(2,1)} %bitcast.188, f32[72,17408]{1,0:T(8,128)} %get-tuple-element.218, pred[]{:T(512)S(6)} %compare.25, bf16[256,72]{0,1:T(8,128)(2,1)S(1)} %select_reduce_fusion.5), kind=kOutput, calls=%fused_computation.2.clone.1 | convolution fusion | flops 644235264 | bytes 18976768 | tf_op jit(solution)/shard_map/while/body/eval_jaxpr/dot_general | solution.py:146
  157.3 7.4 %broadcast_multiply_fusion.2 = bf16[256,136,128]{2,1,0:T(8,128)(2,1)} fusion(bf16[256,128]{1,0:T(8,128)(2,1)S(1)} %dynamic-slice_bitcast_fusion.4, bf16[256,136]{1,0:T(8,128)(2,1)S(1)} %copy.129), kind=kLoop, calls=%fused_computation.5.clone.1 | loop fusion | flops 4456448 | bytes 9048064 | tf_op jit(solution)/shard_map/while/body/eval_jaxpr/mul | solution.py:143
  164.8 9.1 %convolution_add_fusion.10 = f32[72,17408]{1,0:T(8,128)} fusion(bf16[32,8,136,128]{3,2,1,0:T(8,128)(2,1)} %bitcast.188, f32[72,17408]{1,0:T(8,128)} %get-tuple-element.218, pred[]{:T(512)S(6)} %compare.25, bf16[256,72]{0,1:T(8,128)(2,1)S(1)} %select_reduce_fusion.5), kind=kOutput, calls=%fused_computation.2.clone.1 | convolution fusion | flops 644235264 | bytes 18976768 | tf_op jit(solution)/shard_map/while/body/eval_jaxpr/dot_general | solution.py:146
  174.2 7.4 %broadcast_multiply_fusion.2 = bf16[256,136,128]{2,1,0:T(8,128)(2,1)} fusion(bf16[256,128]{1,0:T(8,128)(2,1)S(1)} %dynamic-slice_bitcast_fusion.4, bf16[256,136]{1,0:T(8,128)(2,1)S(1)} %copy.129), kind=kLoop, calls=%fused_computation.5.clone.1 | loop fusion | flops 4456448 | bytes 9048064 | tf_op jit(solution)/shard_map/while/body/eval_jaxpr/mul | solution.py:143
  181.6 9.1 %convolution_add_fusion.10 = f32[72,17408]{1,0:T(8,128)} fusion(bf16[32,8,136,128]{3,2,1,0:T(8,128)(2,1)} %bitcast.188, f32[72,17408]{1,0:T(8,128)} %get-tuple-element.218, pred[]{:T(512)S(6)} %compare.25, bf16[256,72]{0,1:T(8,128)(2,1)S(1)} %select_reduce_fusion.5), kind=kOutput, calls=%fused_computation.2.clone.1 | convolution fusion | flops 644235264 | bytes 18976768 | tf_op jit(solution)/shard_map/while/body/eval_jaxpr/dot_general | solution.py:146
  229.0 5.7 fusion.129
  245.1 396.8 %all-gather.2.cloned.1.call-done = f32[128,3,3,128,128]{4,3,2,1,0:T(8,128)} async-done(((f32[1,3,3,128,128]{4,3,2,1,0:T(8,128)}), f32[128,3,3,128,128]{4,3,2,1,0:T(8,128)}) %all-gather.2.cloned.1.call-update) | async-done | bytes 75497488 | tf_op jit(solution)/shard_map/all_gather | solution.py:198
  641.9 24.1 %reduce_sum.46 = f32[3,3,128,128]{3,2,1,0:T(8,128)} reduce(f32[128,3,3,128,128]{4,3,2,1,0:T(8,128)} %all-gather.2.cloned.1.call-done, f32[]{:T(128)} %constant.170.clone.1), dimensions={0}, to_apply=%region_9.10 | reduce | flops 18726912 | bytes 76087296 | tf_op jit(solution)/shard_map/reduce_sum | solution.py:197
  (191 shorter events, 73.6 us)
Async XLA Ops:
  7.2 7.7 %copy-start.8 = (s32[1024,1]{0,1:T(1,128)S(1)}, s32[1024,1]{0,1:T(1,128)}, u32[]{:S(2)}) copy-start(s32[1024,1]{0,1:T(1,128)} %param.19) | copy-start | bytes 12292
  7.2 7.4 %copy-start.10 = (s32[1024]{0:T(1024)S(1)}, s32[1024]{0:T(1024)}, u32[]{:S(2)}) copy-start(s32[1024]{0:T(1024)} %param.21) | copy-start | bytes 12292
  7.2 7.4 %copy-start.11 = (s32[1024]{0:T(1024)S(1)}, s32[1024]{0:T(1024)}, u32[]{:S(2)}) copy-start(s32[1024]{0:T(1024)} %param.20) | copy-start | bytes 12292
  7.2 7.5 %copy-start.9 = (bf16[1024,2]{0,1:T(2,128)(2,1)S(1)}, bf16[1024,2]{0,1:T(2,128)(2,1)}, u32[]{:S(2)}) copy-start(bf16[1024,2]{0,1:T(2,128)(2,1)} %param.22) | copy-start | bytes 12292
  8.0 36.0 %collective-permute-start.4 = (bf16[1,128,128]{2,1,0:T(8,128)(2,1)S(1)}, bf16[1,128,128]{2,1,0:T(8,128)(2,1)S(1)}, u32[]{:S(2)}, u32[]{:S(2)}) collective-permute-start(bf16[1,128,128]{2,1,0:T(8,128)(2,1)S(1)} %get-tuple-element.169), channel_id=1, source_target_pairs={{0,16},{16,32},{32,48},{48,64},{64,80},{80,96},{96,112},{112,0},{1... | collective-permute-start | bytes 98312 | tf_op jit(solution)/shard_map/ppermute | solution.py:18
  10.1 34.2 %collective-permute-start.5 = (bf16[1,128,128]{2,1,0:T(8,128)(2,1)S(1)}, bf16[1,128,128]{2,1,0:T(8,128)(2,1)S(1)}, u32[]{:S(2)}, u32[]{:S(2)}) collective-permute-start(bf16[1,128,128]{2,1,0:T(8,128)(2,1)S(1)} %get-tuple-element.168), channel_id=1, source_target_pairs={{16,0},{32,16},{48,32},{64,48},{80,64},{96,80},{112,96},{0,112},{1... | collective-permute-start | bytes 98312 | tf_op jit(solution)/shard_map/ppermute | solution.py:20
  15.4 28.6 %copy-start.5 = (bf16[64,128,128]{2,1,0:T(8,128)(2,1)S(1)}, bf16[64,128,128]{2,1,0:T(8,128)(2,1)}, u32[]{:S(2)}) copy-start(bf16[64,128,128]{2,1,0:T(8,128)(2,1)} %param.24) | copy-start | bytes 6291460
  20.3 18.9 %all-to-all-start = ((bf16[128,1,1,16,4]{3,4,2,1,0:T(4,128)(2,1)}), bf16[128,1,1,16,4]{3,4,2,1,0:T(4,128)(2,1)S(1)}, u32[]{:S(2)}, u32[]{:S(2)}) async-start(bf16[128,1,1,16,4]{3,4,2,1,0:T(4,128)(2,1)} %copy.87), calls=%async_computation | async-start | bytes 262144 | tf_op jit(solution)/shard_map/all_to_all | solution.py:44
  39.2 18.0 %all-to-all-start.1 = ((bf16[128,1,1,16,128]{4,3,2,1,0:T(8,128)(2,1)}), bf16[128,1,1,16,128]{4,3,2,1,0:T(8,128)(2,1)S(1)}, u32[]{:S(2)}, u32[]{:S(2)}) async-start(bf16[128,1,1,16,128]{4,3,2,1,0:T(8,128)(2,1)} %bitcast.13), calls=%async_computation.1 | async-start | bytes 1048576 | tf_op jit(solution)/shard_map/all_to_all | solution.py:44
  43.4 598.4 %all-gather.2.cloned.1.call-start = ((), (), s32[]{:S(2)}) async-start(), calls=%async_computation.2 | async-start | bytes 76087296 | tf_op jit(solution)/shard_map/all_gather | solution.py:198
  44.4 1.3 copy-start.3
  45.7 167.7 %collective-permute-start.7 = (bf16[66,1,128]{2,1,0:T(2,128)(2,1)S(1)}, bf16[66,1,128]{2,1,0:T(2,128)(2,1)S(1)}, u32[]{:S(2)}, u32[]{:S(2)}) collective-permute-start(bf16[66,1,128]{2,1,0:T(2,128)(2,1)S(1)} %get-tuple-element.167), channel_id=1, source_target_pairs={{1,0},{2,1},{3,2},{4,3},{5,4},{6,5},{7,6},{8,7},{9,8},{10,9},{11,1... | collective-permute-start | bytes 50696 | tf_op jit(solution)/shard_map/ppermute | solution.py:20
  46.9 166.5 %collective-permute-start.6 = (bf16[66,1,128]{2,1,0:T(2,128)(2,1)S(1)}, bf16[66,1,128]{2,1,0:T(2,128)(2,1)S(1)}, u32[]{:S(2)}, u32[]{:S(2)}) collective-permute-start(bf16[66,1,128]{2,1,0:T(2,128)(2,1)S(1)} %get-tuple-element.166), channel_id=1, source_target_pairs={{0,1},{1,2},{2,3},{3,4},{4,5},{5,6},{6,7},{7,8},{8,9},{9,10},{10,1... | collective-permute-start | bytes 50696 | tf_op jit(solution)/shard_map/ppermute | solution.py:18
  192.0 3.9 copy-start
  196.4 7.5 %collective-permute-start.1 = (bf16[5,136,128]{2,1,0:T(8,128)(2,1)S(1)}, bf16[5,136,128]{2,1,0:T(8,128)(2,1)S(1)}, u32[]{:S(2)}, u32[]{:S(2)}) collective-permute-start(bf16[5,136,128]{2,1,0:T(8,128)(2,1)S(1)} %bitcast.199), channel_id=1, source_target_pairs={{16,0},{32,16},{48,32},{64,48},{80,64},{96,80},{112,96},{17,1},{33... | collective-permute-start | bytes 522248 | tf_op jit(solution)/shard_map/ppermute | solution.py:20
  197.7 7.1 %collective-permute-start = (bf16[5,136,128]{2,1,0:T(8,128)(2,1)S(1)}, bf16[5,136,128]{2,1,0:T(8,128)(2,1)S(1)}, u32[]{:S(2)}, u32[]{:S(2)}) collective-permute-start(bf16[5,136,128]{2,1,0:T(8,128)(2,1)S(1)} %bitcast.203), channel_id=1, source_target_pairs={{0,16},{16,32},{32,48},{48,64},{64,80},{80,96},{96,112},{1,17},{17... | collective-permute-start | bytes 522248 | tf_op jit(solution)/shard_map/ppermute | solution.py:18
  205.3 7.2 %collective-permute-start.3 = (bf16[66,5,128]{2,1,0:T(8,128)(2,1)S(1)}, bf16[66,5,128]{2,1,0:T(8,128)(2,1)S(1)}, u32[]{:S(2)}, u32[]{:S(2)}) collective-permute-start(bf16[66,5,128]{2,1,0:T(8,128)(2,1)S(1)} %get-tuple-element.165), channel_id=1, source_target_pairs={{1,0},{2,1},{3,2},{4,3},{5,4},{6,5},{7,6},{8,7},{9,8},{10,9},{11,1... | collective-permute-start | bytes 253448 | tf_op jit(solution)/shard_map/ppermute | solution.py:20
  206.9 5.5 collective-permute-start.2
  213.0 1.6 copy-start.4
  228.2 0.8 copy-start.6
  229.0 5.7 copy-start.7
  234.7 2.5 copy-start.1
  241.5 1.6 copy-start.2
Sparse Core Ops, SparseCore 0:
  229.1 412.6 all-gather.1
